TPU v7x, 128 devices: a whole 4x4x4 slice. The times are simulated.
128 devices in a mesh: ctx: 16 (over y_hi, z, core), head: 8 (over x, y_lo).
Axes of the slice: x: 4, y: 4 (y_hi: 2, y_lo: 2; y = y_hi * 2 + y_lo), z: 4, core: 2. Of those that a mesh axis runs over, the one named last changes fastest.
Arguments:
- queries: bfloat16 [4096, 8192], P('ctx', 'head'), may hold values from -40 to 40
- keys: bfloat16 [4096, 1024], P('ctx', 'head'), may hold values from -4 to 4
- values: bfloat16 [4096, 1024], P('ctx', 'head'), may hold values from -6 to 6
- out_weight: bfloat16 [8192, 8192], P(None, 'head'), may hold values from -0.1796875 to 0.1796875
- doc_lengths: int32 [16], replicated, may hold values from 1 to 1024, 4096 in all
- owners: int32 [128, 1], replicated, may hold values from 0 to 15; in each aligned block of 8 rows (0 to 7, 8 to 15, ...) no two rows name the same one
Outputs:
- attended: bfloat16 [8192, 8192], P('head', 'ctx')
Inputs may be any that keep to these rules, and one draw needn't show every extreme that they name: `owners`: among the 8 pieces loaded by one index of ctx (aligned blocks of 8 rows) every owner appears at most once. `doc_lengths`: the lengths sum to 4096; the longest is exactly 1024.
All inputs are finite; a program needn't handle non-finite values.
Results may differ from a plain program's by a relative error of at most 0.018.
Values may be sent and summed in bfloat16 or wider, within the bound.
A program may use at most 128 MiB of HBM per device.

v0:
```python
import math

import jax
import jax.numpy as jnp
from jax import lax
from jax.sharding import PartitionSpec as P

HEAD_SIZE = 128
PIECES = 8


MASKED = -1e30


def document_index(positions, doc_starts):
    return jnp.sum((positions[:, None] >= doc_starts[None, :]).astype(jnp.int32), axis=1) - 1


def attend(query_rows, query_pos, keys, values, doc_starts):
    row_count = query_rows.shape[0]
    key_heads = keys.shape[1] // HEAD_SIZE
    group_length = query_rows.shape[1] // keys.shape[1]
    query_heads = query_rows.reshape(row_count, key_heads, group_length, HEAD_SIZE)
    query_doc = document_index(query_pos, doc_starts)
    score_scale = 1.0 / math.sqrt(HEAD_SIZE)
    initial = (
        jnp.full((row_count, key_heads, group_length), MASKED, jnp.float32),
        jnp.zeros((row_count, key_heads, group_length), jnp.float32),
        jnp.zeros((row_count, key_heads, group_length, HEAD_SIZE), jnp.float32),
    )
    key_piece = lax.all_gather(keys, "ctx", axis=0, tiled=True)
    value_piece = lax.all_gather(values, "ctx", axis=0, tiled=True)
    piece_rows = key_piece.shape[0]
    tile_rows = math.gcd(piece_rows, 512)

    def one_tile(tile_index, running):
        tile_start = tile_index * tile_rows
        key_block = lax.dynamic_slice_in_dim(key_piece, tile_start, tile_rows, 0).reshape(
            tile_rows, key_heads, HEAD_SIZE
        )
        value_block = lax.dynamic_slice_in_dim(value_piece, tile_start, tile_rows, 0).reshape(
            tile_rows, key_heads, HEAD_SIZE
        )
        key_pos = tile_start + jnp.arange(tile_rows, dtype=jnp.int32)
        key_doc = document_index(key_pos, doc_starts)
        allowed = (query_doc[:, None] == key_doc[None, :]) & (
            key_pos[None, :] <= query_pos[:, None]
        )
        running_max, running_sum, weighted = running
        scores = (
            jnp.einsum("rkgd,nkd->rkgn", query_heads, key_block, preferred_element_type=jnp.float32)
            * score_scale
        )
        allowed_all = allowed[:, None, None, :]
        scores = jnp.where(allowed_all, scores, MASKED)
        new_max = jnp.maximum(running_max, jnp.max(scores, axis=-1))
        factor = jnp.exp(running_max - new_max)
        weights = jnp.where(allowed_all, jnp.exp(scores - new_max[..., None]), 0.0)
        new_sum = running_sum * factor + jnp.sum(weights, axis=-1)
        new_weighted = weighted * factor[..., None] + jnp.einsum(
            "rkgn,nkd->rkgd",
            weights.astype(jnp.bfloat16),
            value_block,
            preferred_element_type=jnp.float32,
        )
        return (new_max, new_sum, new_weighted)

    final_max, final_sum, weighted = lax.fori_loop(0, piece_rows // tile_rows, one_tile, initial)
    result = weighted / jnp.maximum(final_sum, 1.0)[..., None]
    return result.reshape(row_count, key_heads * group_length * HEAD_SIZE).astype(jnp.bfloat16)


def project(context, out_weight):
    return lax.psum_scatter(
        lax.dot_general(
            out_weight, context, (((1,), (1,)), ((), ())), preferred_element_type=jnp.float32
        ).astype(jnp.bfloat16),
        "head",
        scatter_dimension=0,
        tiled=True,
    )


def per_device(queries, keys, values, out_weight, doc_lengths, owners):
    place_count = lax.axis_size("ctx")
    own_index = lax.axis_index("ctx")
    token_count = queries.shape[0]
    block_rows = token_count // PIECES
    doc_ends = jnp.cumsum(doc_lengths)
    doc_starts = doc_ends - doc_lengths
    owner_table = owners[:, 0].reshape(place_count, PIECES)
    own_owners = lax.dynamic_index_in_dim(owner_table, own_index, 0, keepdims=False)
    place_ids = jnp.arange(place_count, dtype=jnp.int32)
    send_pick = (own_owners[None, :] == place_ids[:, None]).astype(jnp.bfloat16)
    grouped = queries.reshape(PIECES, block_rows, queries.shape[1])
    outgoing = jnp.einsum(
        "oc,chw->ohw", send_pick, grouped, preferred_element_type=jnp.float32
    ).astype(jnp.bfloat16)
    arrived = lax.all_to_all(outgoing, "ctx", split_axis=0, concat_axis=0, tiled=True)
    slot_hits = (owner_table == own_index).astype(jnp.int32)
    slot_live = jnp.sum(slot_hits, axis=1)
    picked = jnp.sum(slot_hits * jnp.arange(PIECES, dtype=jnp.int32)[None, :], axis=1)
    slot_pos = (place_ids[:, None] * PIECES + picked[:, None]) * block_rows + jnp.arange(
        block_rows, dtype=jnp.int32
    )[None, :]
    query_pos = jnp.where(slot_live[:, None] > 0, slot_pos, -1).reshape(-1)
    context = attend(
        arrived.reshape(place_count * block_rows, queries.shape[1]),
        query_pos,
        keys,
        values,
        doc_starts,
    )
    return project(context, out_weight)


def solution(mesh):
    in_specs = (P("ctx", "head"), P("ctx", "head"), P("ctx", "head"), P(None, "head"), P(), P())
    out_specs = P("head", "ctx")
    return jax.shard_map(
        per_device, mesh=mesh, in_specs=in_specs, out_specs=out_specs, check_vma=False
    )
```

profile of v0, /device:TPU:1, one launch (start us, length us, event | category | flops | bytes accessed | tf_op | source)
XLA Modules:
  0.0 447.8 jit_solution(8140803811860141464)
XLA Ops:
  6.5 1.6 copy.30
  8.2 0.7 all-gather.3.cloned.1.call-update
  8.9 0.5 broadcast.215
  9.5 1.3 reduce.16
  10.8 0.1 reshape_squeeze.3
  10.9 0.6 convolution_convert_fusion.1
  11.5 1.5 copy.29
  13.0 9.5 %all-to-all-start = ((bf16[16,32,1024]{2,1,0:T(8,128)(2,1)}), bf16[16,32,1024]{2,1,0:T(8,128)(2,1)S(1)}, u32[]{:S(2)}, u32[]{:S(2)}) async-start(bf16[16,32,1024]{2,1,0:T(8,128)(2,1)} %copy.29), calls=%async_computation | async-start | bytes 2097152 | tf_op jit(solution)/shard_map/all_to_all | solution.py:99
  22.5 0.1 convert_reduce_fusion.2
  22.8 0.7 copy.27
  23.6 0.1 reduce.13
  23.7 0.7 sub.49
  24.4 0.1 convert_reduce_fusion.1
  24.5 15.9 %all-to-all-done = bf16[16,32,1024]{2,1,0:T(8,128)(2,1)S(1)} async-done(((bf16[16,32,1024]{2,1,0:T(8,128)(2,1)}), bf16[16,32,1024]{2,1,0:T(8,128)(2,1)S(1)}, u32[]{:S(2)}, u32[]{:S(2)}) %all-to-all-start) | async-done | bytes 1048608 | tf_op jit(solution)/shard_map/all_to_all | solution.py:99
  40.4 0.3 copy.34
  40.7 0.1 copy.31
  40.8 20.1 %all-gather.5.cloned.1.call-done = bf16[4096,128]{0,1:T(8,128)(2,1)} async-done(((bf16[256,128]{0,1:T(8,128)(2,1)}), bf16[4096,128]{0,1:T(8,128)(2,1)}) %all-gather.5.cloned.1.call-update) | async-done | bytes 1048592 | tf_op jit(solution)/shard_map/all_gather | solution.py:32
  60.9 47.4 %all-gather.3.cloned.1.call-done = bf16[4096,128]{1,0:T(8,128)(2,1)} async-done(((bf16[256,128]{1,0:T(8,128)(2,1)}), bf16[4096,128]{1,0:T(8,128)(2,1)}) %all-gather.3.cloned.1.call-update) | async-done | bytes 1048592 | tf_op jit(solution)/shard_map/all_gather | solution.py:31
  108.2 131.5 %while.20 = (s32[]{:T(128)}, f32[512,1,8]{0,2,1:T(8,128)S(1)}, f32[512,1,8]{0,2,1:T(8,128)S(1)}, f32[512,1,8,128]{0,3,2,1:T(8,128)}, s32[512]{0:T(512)S(1)}, /*i...) while((s32[]{:T(128)}, f32[512,1,8]{0,2,1:T(8,128)S(1)}, ...), condition=%wide.region_8.9_spmd.clone, body=%wide.region_4.8_spmd.clone.sunk | while | flops 1103414784 | bytes 65560956 | solution.py:68
  108.2 0.1 convert_reduce_fusion.4
  108.5 0.3 compare_and_fusion.2
  108.8 5.6 %fusion.37 = (f32[512,8]{0,1:T(8,128)S(1)}, f32[512,512,8]{1,0,2:T(8,128)}) fusion(pred[512,512]{0,1:T(8,128)(4,1)S(1)} %compare_and_fusion.2, bf16[512,1,8,128]{3,0,2,1:T(8,128)(2,1)S(1)} %get-tuple-element.463, bf16[4096,128]{1,0:T(8,128)(2,1)} %get-tuple-element.462, s32[]{:T(128)S(6)} %select_n.96), kind=kOutput, calls=%fused_computation.3.clone.1 | convolution fusion | flops 543158272 | bytes 9846788 | tf_op jit(solution)/shard_map/while/body/eval_jaxpr/rkgd,nkd->rkgn/dot_general | solution.py:51
  114.4 7.6 %bitcast_add_fusion.5 = f32[512,1,8,128]{0,3,2,1:T(8,128)} fusion(f32[512,1,8,128]{0,3,2,1:T(8,128)} %get-tuple-element.444, f32[512,512,8]{1,0,2:T(8,128)} %get-tuple-element.424, f32[512,8]{0,1:T(8,128)S(1)} %bitcast.90, pred[512,512]{0,1:T(8,128)(4,1)S(1)} %compare_and_fusion.2, f32[512,8]{0,1:T(8,128)S(1)} %get-tuple-element.425, ...), kind=kOutput, calls=%fused_computation.9.clone.1 | convolution fusion | flops 548929536 | bytes 13008901 | tf_op jit(solution)/shard_map/while/body/eval_jaxpr/rkgn,nkd->rkgd/dot_general | solution.py:60
  122.1 2.0 fusion.39
  124.1 0.1 convert_reduce_fusion.4
  124.3 0.1 le.52
  124.4 0.3 compare_and_fusion.2
  124.7 5.6 %fusion.37 = (f32[512,8]{0,1:T(8,128)S(1)}, f32[512,512,8]{1,0,2:T(8,128)}) fusion(pred[512,512]{0,1:T(8,128)(4,1)S(1)} %compare_and_fusion.2, bf16[512,1,8,128]{3,0,2,1:T(8,128)(2,1)S(1)} %get-tuple-element.463, bf16[4096,128]{1,0:T(8,128)(2,1)} %get-tuple-element.462, s32[]{:T(128)S(6)} %select_n.96), kind=kOutput, calls=%fused_computation.3.clone.1 | convolution fusion | flops 543158272 | bytes 9846788 | tf_op jit(solution)/shard_map/while/body/eval_jaxpr/rkgd,nkd->rkgn/dot_general | solution.py:51
  130.3 8.2 %bitcast_add_fusion.5 = f32[512,1,8,128]{0,3,2,1:T(8,128)} fusion(f32[512,1,8,128]{0,3,2,1:T(8,128)} %get-tuple-element.444, f32[512,512,8]{1,0,2:T(8,128)} %get-tuple-element.424, f32[512,8]{0,1:T(8,128)S(1)} %bitcast.90, pred[512,512]{0,1:T(8,128)(4,1)S(1)} %compare_and_fusion.2, f32[512,8]{0,1:T(8,128)S(1)} %get-tuple-element.425, ...), kind=kOutput, calls=%fused_computation.9.clone.1 | convolution fusion | flops 548929536 | bytes 13008901 | tf_op jit(solution)/shard_map/while/body/eval_jaxpr/rkgn,nkd->rkgd/dot_general | solution.py:60
  138.6 2.0 fusion.39
  140.7 0.1 convert_reduce_fusion.4
  140.9 0.3 compare_and_fusion.2
  141.2 5.6 %fusion.37 = (f32[512,8]{0,1:T(8,128)S(1)}, f32[512,512,8]{1,0,2:T(8,128)}) fusion(pred[512,512]{0,1:T(8,128)(4,1)S(1)} %compare_and_fusion.2, bf16[512,1,8,128]{3,0,2,1:T(8,128)(2,1)S(1)} %get-tuple-element.463, bf16[4096,128]{1,0:T(8,128)(2,1)} %get-tuple-element.462, s32[]{:T(128)S(6)} %select_n.96), kind=kOutput, calls=%fused_computation.3.clone.1 | convolution fusion | flops 543158272 | bytes 9846788 | tf_op jit(solution)/shard_map/while/body/eval_jaxpr/rkgd,nkd->rkgn/dot_general | solution.py:51
  146.8 8.2 %bitcast_add_fusion.5 = f32[512,1,8,128]{0,3,2,1:T(8,128)} fusion(f32[512,1,8,128]{0,3,2,1:T(8,128)} %get-tuple-element.444, f32[512,512,8]{1,0,2:T(8,128)} %get-tuple-element.424, f32[512,8]{0,1:T(8,128)S(1)} %bitcast.90, pred[512,512]{0,1:T(8,128)(4,1)S(1)} %compare_and_fusion.2, f32[512,8]{0,1:T(8,128)S(1)} %get-tuple-element.425, ...), kind=kOutput, calls=%fused_computation.9.clone.1 | convolution fusion | flops 548929536 | bytes 13008901 | tf_op jit(solution)/shard_map/while/body/eval_jaxpr/rkgn,nkd->rkgd/dot_general | solution.py:60
  155.1 2.0 fusion.39
  157.2 0.1 convert_reduce_fusion.4
  157.4 0.3 compare_and_fusion.2
  157.7 5.6 %fusion.37 = (f32[512,8]{0,1:T(8,128)S(1)}, f32[512,512,8]{1,0,2:T(8,128)}) fusion(pred[512,512]{0,1:T(8,128)(4,1)S(1)} %compare_and_fusion.2, bf16[512,1,8,128]{3,0,2,1:T(8,128)(2,1)S(1)} %get-tuple-element.463, bf16[4096,128]{1,0:T(8,128)(2,1)} %get-tuple-element.462, s32[]{:T(128)S(6)} %select_n.96), kind=kOutput, calls=%fused_computation.3.clone.1 | convolution fusion | flops 543158272 | bytes 9846788 | tf_op jit(solution)/shard_map/while/body/eval_jaxpr/rkgd,nkd->rkgn/dot_general | solution.py:51
  163.3 8.2 %bitcast_add_fusion.5 = f32[512,1,8,128]{0,3,2,1:T(8,128)} fusion(f32[512,1,8,128]{0,3,2,1:T(8,128)} %get-tuple-element.444, f32[512,512,8]{1,0,2:T(8,128)} %get-tuple-element.424, f32[512,8]{0,1:T(8,128)S(1)} %bitcast.90, pred[512,512]{0,1:T(8,128)(4,1)S(1)} %compare_and_fusion.2, f32[512,8]{0,1:T(8,128)S(1)} %get-tuple-element.425, ...), kind=kOutput, calls=%fused_computation.9.clone.1 | convolution fusion | flops 548929536 | bytes 13008901 | tf_op jit(solution)/shard_map/while/body/eval_jaxpr/rkgn,nkd->rkgd/dot_general | solution.py:60
  171.6 2.0 fusion.39
  173.7 0.1 convert_reduce_fusion.4
  173.9 0.3 compare_and_fusion.2
  174.2 5.6 %fusion.37 = (f32[512,8]{0,1:T(8,128)S(1)}, f32[512,512,8]{1,0,2:T(8,128)}) fusion(pred[512,512]{0,1:T(8,128)(4,1)S(1)} %compare_and_fusion.2, bf16[512,1,8,128]{3,0,2,1:T(8,128)(2,1)S(1)} %get-tuple-element.463, bf16[4096,128]{1,0:T(8,128)(2,1)} %get-tuple-element.462, s32[]{:T(128)S(6)} %select_n.96), kind=kOutput, calls=%fused_computation.3.clone.1 | convolution fusion | flops 543158272 | bytes 9846788 | tf_op jit(solution)/shard_map/while/body/eval_jaxpr/rkgd,nkd->rkgn/dot_general | solution.py:51
  179.9 8.2 %bitcast_add_fusion.5 = f32[512,1,8,128]{0,3,2,1:T(8,128)} fusion(f32[512,1,8,128]{0,3,2,1:T(8,128)} %get-tuple-element.444, f32[512,512,8]{1,0,2:T(8,128)} %get-tuple-element.424, f32[512,8]{0,1:T(8,128)S(1)} %bitcast.90, pred[512,512]{0,1:T(8,128)(4,1)S(1)} %compare_and_fusion.2, f32[512,8]{0,1:T(8,128)S(1)} %get-tuple-element.425, ...), kind=kOutput, calls=%fused_computation.9.clone.1 | convolution fusion | flops 548929536 | bytes 13008901 | tf_op jit(solution)/shard_map/while/body/eval_jaxpr/rkgn,nkd->rkgd/dot_general | solution.py:60
  188.1 2.0 fusion.39
  190.2 0.1 convert_reduce_fusion.4
  190.4 0.3 compare_and_fusion.2
  190.7 5.6 %fusion.37 = (f32[512,8]{0,1:T(8,128)S(1)}, f32[512,512,8]{1,0,2:T(8,128)}) fusion(pred[512,512]{0,1:T(8,128)(4,1)S(1)} %compare_and_fusion.2, bf16[512,1,8,128]{3,0,2,1:T(8,128)(2,1)S(1)} %get-tuple-element.463, bf16[4096,128]{1,0:T(8,128)(2,1)} %get-tuple-element.462, s32[]{:T(128)S(6)} %select_n.96), kind=kOutput, calls=%fused_computation.3.clone.1 | convolution fusion | flops 543158272 | bytes 9846788 | tf_op jit(solution)/shard_map/while/body/eval_jaxpr/rkgd,nkd->rkgn/dot_general | solution.py:51
  196.4 8.2 %bitcast_add_fusion.5 = f32[512,1,8,128]{0,3,2,1:T(8,128)} fusion(f32[512,1,8,128]{0,3,2,1:T(8,128)} %get-tuple-element.444, f32[512,512,8]{1,0,2:T(8,128)} %get-tuple-element.424, f32[512,8]{0,1:T(8,128)S(1)} %bitcast.90, pred[512,512]{0,1:T(8,128)(4,1)S(1)} %compare_and_fusion.2, f32[512,8]{0,1:T(8,128)S(1)} %get-tuple-element.425, ...), kind=kOutput, calls=%fused_computation.9.clone.1 | convolution fusion | flops 548929536 | bytes 13008901 | tf_op jit(solution)/shard_map/while/body/eval_jaxpr/rkgn,nkd->rkgd/dot_general | solution.py:60
  204.6 2.0 fusion.39
  206.7 0.1 convert_reduce_fusion.4
  207.0 0.3 compare_and_fusion.2
  207.2 5.6 %fusion.37 = (f32[512,8]{0,1:T(8,128)S(1)}, f32[512,512,8]{1,0,2:T(8,128)}) fusion(pred[512,512]{0,1:T(8,128)(4,1)S(1)} %compare_and_fusion.2, bf16[512,1,8,128]{3,0,2,1:T(8,128)(2,1)S(1)} %get-tuple-element.463, bf16[4096,128]{1,0:T(8,128)(2,1)} %get-tuple-element.462, s32[]{:T(128)S(6)} %select_n.96), kind=kOutput, calls=%fused_computation.3.clone.1 | convolution fusion | flops 543158272 | bytes 9846788 | tf_op jit(solution)/shard_map/while/body/eval_jaxpr/rkgd,nkd->rkgn/dot_general | solution.py:51
  212.9 8.2 %bitcast_add_fusion.5 = f32[512,1,8,128]{0,3,2,1:T(8,128)} fusion(f32[512,1,8,128]{0,3,2,1:T(8,128)} %get-tuple-element.444, f32[512,512,8]{1,0,2:T(8,128)} %get-tuple-element.424, f32[512,8]{0,1:T(8,128)S(1)} %bitcast.90, pred[512,512]{0,1:T(8,128)(4,1)S(1)} %compare_and_fusion.2, f32[512,8]{0,1:T(8,128)S(1)} %get-tuple-element.425, ...), kind=kOutput, calls=%fused_computation.9.clone.1 | convolution fusion | flops 548929536 | bytes 13008901 | tf_op jit(solution)/shard_map/while/body/eval_jaxpr/rkgn,nkd->rkgd/dot_general | solution.py:60
  221.1 2.0 fusion.39
  223.2 0.1 convert_reduce_fusion.4
  223.5 0.3 compare_and_fusion.2
  223.8 5.6 %fusion.37 = (f32[512,8]{0,1:T(8,128)S(1)}, f32[512,512,8]{1,0,2:T(8,128)}) fusion(pred[512,512]{0,1:T(8,128)(4,1)S(1)} %compare_and_fusion.2, bf16[512,1,8,128]{3,0,2,1:T(8,128)(2,1)S(1)} %get-tuple-element.463, bf16[4096,128]{1,0:T(8,128)(2,1)} %get-tuple-element.462, s32[]{:T(128)S(6)} %select_n.96), kind=kOutput, calls=%fused_computation.3.clone.1 | convolution fusion | flops 543158272 | bytes 9846788 | tf_op jit(solution)/shard_map/while/body/eval_jaxpr/rkgd,nkd->rkgn/dot_general | solution.py:51
  229.4 8.2 %bitcast_add_fusion.5 = f32[512,1,8,128]{0,3,2,1:T(8,128)} fusion(f32[512,1,8,128]{0,3,2,1:T(8,128)} %get-tuple-element.444, f32[512,512,8]{1,0,2:T(8,128)} %get-tuple-element.424, f32[512,8]{0,1:T(8,128)S(1)} %bitcast.90, pred[512,512]{0,1:T(8,128)(4,1)S(1)} %compare_and_fusion.2, f32[512,8]{0,1:T(8,128)S(1)} %get-tuple-element.425, ...), kind=kOutput, calls=%fused_computation.9.clone.1 | convolution fusion | flops 548929536 | bytes 13008901 | tf_op jit(solution)/shard_map/while/body/eval_jaxpr/rkgn,nkd->rkgd/dot_general | solution.py:60
  237.7 2.0 fusion.39
  239.7 1.9 divide_convert_fusion
  241.6 29.8 %fusion.23 = bf16[8192,512]{0,1:T(8,128)(2,1)} fusion(bf16[512,1024]{0,1:T(8,128)(2,1)S(1)} %bitcast.94, bf16[8192,1024]{1,0:T(8,128)(2,1)} %param.11), kind=kOutput, calls=%fused_computation.33 | convolution fusion | flops 8594128896 | bytes 26214400 | tf_op jit(solution)/shard_map/dot_general | solution.py:75
  271.5 167.6 %reduce-scatter.2.cloned.1.call-done = bf16[1024,512]{0,1:T(8,128)(2,1)} async-done(((bf16[8192,512]{0,1:T(8,128)(2,1)}), bf16[1024,512]{0,1:T(8,128)(2,1)}) %reduce-scatter.2.cloned.1.call-update) | async-done | bytes 1048592 | tf_op jit(solution)/shard_map/reduce_scatter | solution.py:74
  439.0 2.3 copy.32
  (89 shorter events, 1.8 us)
Async XLA Ops:
  6.5 4.3 copy-start
  6.5 54.3 %all-gather.5.cloned.1.call-start = ((), (), s32[]{:S(2)}) async-start(), calls=%async_computation.3 | async-start | bytes 1114112 | tf_op jit(solution)/shard_map/all_gather | solution.py:32
  8.2 100.0 %all-gather.3.cloned.1.call-start = ((), (), s32[]{:S(2)}) async-start(), calls=%async_computation.2 | async-start | bytes 1114112 | tf_op jit(solution)/shard_map/all_gather | solution.py:31
  13.0 27.4 %all-to-all-start = ((bf16[16,32,1024]{2,1,0:T(8,128)(2,1)}), bf16[16,32,1024]{2,1,0:T(8,128)(2,1)S(1)}, u32[]{:S(2)}, u32[]{:S(2)}) async-start(bf16[16,32,1024]{2,1,0:T(8,128)(2,1)} %copy.29), calls=%async_computation | async-start | bytes 2097152 | tf_op jit(solution)/shard_map/all_to_all | solution.py:99
  22.5 416.6 %reduce-scatter.2.cloned.1.call-start = ((), (), s32[]{:S(2)}) async-start(), calls=%async_computation.4 | async-start | bytes 9437184 | tf_op jit(solution)/shard_map/reduce_scatter | solution.py:74
  114.4 7.7 %copy-start.1 = (f32[512,512,8]{1,0,2:T(8,128)S(1)}, f32[512,512,8]{1,0,2:T(8,128)}, u32[]{:S(2)}) copy-start(f32[512,512,8]{1,0,2:T(8,128)} %get-tuple-element.424) | copy-start | bytes 25165828 | tf_op jit(solution)/shard_map/while
  130.3 8.3 %copy-start.1 = (f32[512,512,8]{1,0,2:T(8,128)S(1)}, f32[512,512,8]{1,0,2:T(8,128)}, u32[]{:S(2)}) copy-start(f32[512,512,8]{1,0,2:T(8,128)} %get-tuple-element.424) | copy-start | bytes 25165828 | tf_op jit(solution)/shard_map/while
  146.8 8.3 %copy-start.1 = (f32[512,512,8]{1,0,2:T(8,128)S(1)}, f32[512,512,8]{1,0,2:T(8,128)}, u32[]{:S(2)}) copy-start(f32[512,512,8]{1,0,2:T(8,128)} %get-tuple-element.424) | copy-start | bytes 25165828 | tf_op jit(solution)/shard_map/while
  163.3 8.3 %copy-start.1 = (f32[512,512,8]{1,0,2:T(8,128)S(1)}, f32[512,512,8]{1,0,2:T(8,128)}, u32[]{:S(2)}) copy-start(f32[512,512,8]{1,0,2:T(8,128)} %get-tuple-element.424) | copy-start | bytes 25165828 | tf_op jit(solution)/shard_map/while
  179.8 8.3 %copy-start.1 = (f32[512,512,8]{1,0,2:T(8,128)S(1)}, f32[512,512,8]{1,0,2:T(8,128)}, u32[]{:S(2)}) copy-start(f32[512,512,8]{1,0,2:T(8,128)} %get-tuple-element.424) | copy-start | bytes 25165828 | tf_op jit(solution)/shard_map/while
  196.4 8.3 %copy-start.1 = (f32[512,512,8]{1,0,2:T(8,128)S(1)}, f32[512,512,8]{1,0,2:T(8,128)}, u32[]{:S(2)}) copy-start(f32[512,512,8]{1,0,2:T(8,128)} %get-tuple-element.424) | copy-start | bytes 25165828 | tf_op jit(solution)/shard_map/while
  212.9 8.3 %copy-start.1 = (f32[512,512,8]{1,0,2:T(8,128)S(1)}, f32[512,512,8]{1,0,2:T(8,128)}, u32[]{:S(2)}) copy-start(f32[512,512,8]{1,0,2:T(8,128)} %get-tuple-element.424) | copy-start | bytes 25165828 | tf_op jit(solution)/shard_map/while
  229.4 8.3 %copy-start.1 = (f32[512,512,8]{1,0,2:T(8,128)S(1)}, f32[512,512,8]{1,0,2:T(8,128)}, u32[]{:S(2)}) copy-start(f32[512,512,8]{1,0,2:T(8,128)} %get-tuple-element.424) | copy-start | bytes 25165828 | tf_op jit(solution)/shard_map/while
Sparse Core Ops, SparseCore 0:
  9.6 51.1 all-gather.4
  63.3 44.8 all-gather.2
  271.6 167.4 reduce-scatter.1
where the time goes:
time: 448 us
  waiting for transfers between devices  252 us (56%)
  matrix products  141 us (31%)
  other arithmetic  24.2 us (5%)
  between operations  13.2 us (3%)
  starting transfers between devices  9.54 us (2%)
  local copies, waits for them, and re-layouts  7.97 us (2%)
    reduce_scatter x1, waiting for transfers between devices, project(): lax.psum_scatter(lax.dot_general(out_weight, context, (((1,), (1,)), ((),...  168 us
    dot_general x8, matrix products, one_tile(): jnp.einsum('rkgn,nkd->rkgd', weights.astype(jnp.bfloat16), value_block, p...  65.4 us
    all_gather x1, waiting for transfers between devices, attend(): key_piece = lax.all_gather(keys, 'ctx', axis=0, tiled=True)  47.4 us
    dot_general x8, matrix products, one_tile(): jnp.einsum('rkgd,nkd->rkgn', query_heads, key_block, preferred_element_ty...  44.9 us
    dot_general x1, matrix products, project(): lax.dot_general(out_weight, context, (((1,), (1,)), ((), ())), preferred_...  29.8 us
    all_gather x1, waiting for transfers between devices, attend(): value_piece = lax.all_gather(values, 'ctx', axis=0, tiled=True)  20.1 us
    reduce_sum x8, other arithmetic, one_tile(): new_sum = running_sum * factor + jnp.sum(weights, axis=-1)  16.1 us
    all_to_all x1, waiting for transfers between devices, per_device(): lax.all_to_all(outgoing, 'ctx', split_axis=0, concat_axis=0, tiled=True)  15.9 us
  transfers between devices with their start and end apart: 4, of which 4 were waited for; matrix products, arithmetic and copies ran while one was open for 1% of the time, Pallas kernels for 0%

commit v1 on v0

v1 whole, which is shorter than its diff:
```python
import functools
import math

import jax
import jax.numpy as jnp
from jax import lax
from jax.experimental import pallas as pl
from jax.experimental.pallas import tpu as pltpu
from jax.sharding import PartitionSpec as P

HEAD_SIZE = 128
PIECES = 8
PIECE = 32
NDOC = 16
N_CTX = 16
N_X = 4
ROWS = 256
HEADS = 8
BACK = 4
KEYS = (BACK + 1) * ROWS
CHUNKS = 4
CHUNK = 256
HALF = 128
MASKED = -1e30
VMEM_LIMIT = 60 * 1024 * 1024


def signal(sem, **where):
    pl.semaphore_signal(
        sem, inc=1, device_id=where, device_id_type=pl.DeviceIdType.MESH
    )


def remote(src, dst, send_sem, recv_sem, **where):
    return pltpu.make_async_remote_copy(
        src_ref=src,
        dst_ref=dst,
        send_sem=send_sem,
        recv_sem=recv_sem,
        device_id=where,
        device_id_type=pl.DeviceIdType.MESH,
    )


def attention_kernel(
    lengths, q_ref, k_ref, v_ref, o_ref, kbuf, vbuf, vt, bias, send_sem, recv_sem
):
    c = lax.axis_index("ctx")
    core = lax.rem(c, 2)
    mate = c + 1 - 2 * core

    barrier = pltpu.get_barrier_semaphore()
    signal(barrier, ctx=mate)
    for far in (2, 4):

        @pl.when(c + far < N_CTX)
        def _():
            signal(barrier, ctx=c + far)

        @pl.when(c >= far)
        def _():
            signal(barrier, ctx=c - far)

    def slot(buf, back):
        return buf.at[pl.ds((BACK - back) * ROWS, ROWS)]

    kbuf[BACK * ROWS :, :] = k_ref[...]
    vbuf[BACK * ROWS :, :] = v_ref[...]
    for back in range(1, BACK + 1):

        @pl.when(c < back)
        def _():
            at = (BACK - back) * ROWS
            kbuf[at : at + ROWS, :] = jnp.zeros((ROWS, HEAD_SIZE), jnp.bfloat16)
            vbuf[at : at + ROWS, :] = jnp.zeros((ROWS, HEAD_SIZE), jnp.bfloat16)

    pos = c * ROWS + lax.broadcasted_iota(jnp.int32, (1, ROWS), 1)
    begin = jnp.int32(0)
    low = jnp.zeros((1, ROWS), jnp.int32)
    for doc in range(NDOC):
        low = jnp.where(pos >= begin, begin, low)
        begin = begin + lengths[doc]
    for at in range(0, KEYS, ROWS):
        key_pos = (
            (c - BACK) * ROWS
            + at
            + lax.broadcasted_iota(jnp.int32, (ROWS, ROWS), 0)
        )
        allowed = (key_pos >= low) & (key_pos <= pos)
        bias[at : at + ROWS, :] = jnp.where(allowed, 0.0, MASKED)

    count = 1
    for far in (2, 4):
        count = count + (c + far < N_CTX).astype(jnp.int32)
        count = count + (c >= far).astype(jnp.int32)
    pl.semaphore_wait(barrier, count)

    def far_copies(far):
        return [
            remote(
                own,
                slot(buf, far),
                send_sem.at[far // 2 - 1, i],
                recv_sem.at[far - 1, i],
                ctx=c + far,
            )
            for i, (own, buf) in enumerate(((k_ref, kbuf), (v_ref, vbuf)))
        ]

    def mate_copies(source, back):
        return [
            remote(
                source[i],
                slot(buf, back),
                send_sem.at[2 + back // 2, i],
                recv_sem.at[back - 1, i],
                ctx=mate,
            )
            for i, buf in enumerate((kbuf, vbuf))
        ]

    first_even = mate_copies((k_ref, v_ref), 1)
    first_odd = mate_copies((slot(kbuf, 2), slot(vbuf, 2)), 1)
    second_even = mate_copies((slot(kbuf, 2), slot(vbuf, 2)), 3)
    second_odd = mate_copies((slot(kbuf, 4), slot(vbuf, 4)), 3)

    @pl.when(core == 0)
    def _():
        for copy in first_even:
            copy.start()

    for far in (2, 4):

        @pl.when(c + far < N_CTX)
        def _():
            for copy in far_copies(far):
                copy.start()

    @pl.when(c >= 2)
    def _():
        for copy in far_copies(2):
            copy.wait_recv()

        @pl.when(core == 1)
        def _():
            for copy in first_odd:
                copy.start()

        @pl.when(core == 0)
        def _():
            for copy in second_even:
                copy.start()

    @pl.when(c >= 4)
    def _():
        for copy in far_copies(4):
            copy.wait_recv()

        @pl.when(core == 1)
        def _():
            for copy in second_odd:
                copy.start()

    @pl.when(c >= 1)
    def _():
        for copy in first_odd:
            copy.wait_recv()

    @pl.when(c >= 3)
    def _():
        for copy in second_odd:
            copy.wait_recv()

    vt[...] = vbuf[...].T
    factor = math.log2(math.e) / math.sqrt(HEAD_SIZE)

    @pl.loop(0, HEADS)
    def _(head):
        at = pl.multiple_of(head * HEAD_SIZE, HEAD_SIZE)
        scores = lax.dot_general(
            kbuf[...],
            q_ref[:, pl.ds(at, HEAD_SIZE)],
            (((1,), (1,)), ((), ())),
            preferred_element_type=jnp.float32,
        )
        scores = scores + bias[...]
        top = jnp.max(scores, axis=0, keepdims=True)
        weights = jnp.exp2((scores - top) * factor)
        total = jnp.sum(weights, axis=0, keepdims=True)
        mixed = jnp.dot(
            vt[...], weights.astype(jnp.bfloat16), preferred_element_type=jnp.float32
        )
        o_ref[pl.ds(at, HEAD_SIZE), :] = (mixed / total).astype(jnp.bfloat16)

    for far in (2, 4):

        @pl.when(c + far < N_CTX)
        def _():
            for copy in far_copies(far):
                copy.wait_send()

    @pl.when(core == 0)
    def _():
        for copy in first_even:
            copy.wait_send()

        @pl.when(c >= 2)
        def _():
            for copy in second_even:
                copy.wait_send()

    @pl.when(core == 1)
    def _():
        @pl.when(c >= 2)
        def _():
            for copy in first_odd:
                copy.wait_send()

        @pl.when(c >= 4)
        def _():
            for copy in second_odd:
                copy.wait_send()


def attention(lengths, queries, keys, values):
    vmem = pl.BlockSpec(memory_space=pltpu.VMEM)
    return pl.pallas_call(
        attention_kernel,
        out_shape=jax.ShapeDtypeStruct((HEADS * HEAD_SIZE, ROWS), jnp.bfloat16),
        in_specs=[pl.BlockSpec(memory_space=pltpu.SMEM), vmem, vmem, vmem],
        out_specs=vmem,
        scratch_shapes=[
            pltpu.VMEM((KEYS, HEAD_SIZE), jnp.bfloat16),
            pltpu.VMEM((KEYS, HEAD_SIZE), jnp.bfloat16),
            pltpu.VMEM((HEAD_SIZE, KEYS), jnp.bfloat16),
            pltpu.VMEM((KEYS, ROWS), jnp.float32),
            pltpu.SemaphoreType.DMA((4, 2)),
            pltpu.SemaphoreType.DMA((4, 2)),
        ],
        compiler_params=pltpu.CompilerParams(
            collective_id=0, has_side_effects=True, vmem_limit_bytes=VMEM_LIMIT
        ),
        name="attention",
    )(lengths, queries, keys, values)


def project_kernel(
    owners,
    w_ref,
    ctx_ref,
    out_ref,
    weights,
    partial,
    far_buf,
    near_buf,
    side_buf,
    near_out,
    cross_out,
    cross_buf,
    keep,
    pick,
    slab,
    w_sem,
    far_sem,
    near_sem,
    side_sem,
    cross_sem,
    spread_sem,
):
    c = lax.axis_index("ctx")
    h = lax.axis_index("head")
    x = h // 2
    y = lax.rem(h, 2)

    def column(step):
        return lax.rem(x + step + N_X, N_X)

    def at_x(step):
        return column(step) * 2 + y

    other = x * 2 + 1 - y

    barrier = pltpu.get_barrier_semaphore()
    for step in (1, -1):
        signal(barrier, head=at_x(step))
    signal(barrier, head=other)
    for step in range(1, N_CTX):
        signal(barrier, ctx=lax.rem(c + step, N_CTX))

    def load(place, i):
        return pltpu.make_async_copy(
            w_ref.at[place, :, i], weights.at[place, i], w_sem.at[place, i]
        )

    for step in (2, 1, -1, 0):
        for i in range(CHUNKS):
            load(column(step), i).start()

    row = lax.broadcasted_iota(jnp.int32, (N_CTX * PIECE, ROWS), 0)
    col = lax.broadcasted_iota(jnp.int32, (N_CTX * PIECE, ROWS), 1)
    lane = lax.broadcasted_iota(jnp.int32, (1, ROWS), 1)
    wanted = jnp.zeros((1, ROWS), jnp.int32)
    for piece in range(PIECES):
        wanted = jnp.where(
            (lane >= piece * PIECE) & (lane < (piece + 1) * PIECE),
            owners[c * PIECES + piece] * PIECE + lane - piece * PIECE,
            wanted,
        )
    pick[...] = (row == wanted).astype(jnp.float32).astype(jnp.bfloat16)

    def multiply(step, i):
        place = column(step)
        load(place, i).wait()

        @pl.loop(0, 2)
        def _(side):
            block = jnp.dot(
                weights[place, i, side],
                ctx_ref[...],
                preferred_element_type=jnp.float32,
            ).astype(jnp.bfloat16)
            partial[place, i, 0, side] = block[:HALF]
            partial[place, i, 1, side] = block[HALF:]

    def toward(u):
        return 2 * u - 1

    def far_copy(i, u):
        return remote(
            partial.at[column(2), i, u],
            far_buf.at[i, u],
            far_sem.at[0, i, u],
            far_sem.at[1, i, u],
            head=at_x(toward(u)),
        )

    def side_copy(i, u):
        return remote(
            partial.at[column(-toward(u)), i, u],
            side_buf.at[i, u],
            side_sem.at[0, i, u],
            side_sem.at[1, i, u],
            head=at_x(-toward(u)),
        )

    def near_copy(i, u):
        return remote(
            near_out.at[i, u],
            near_buf.at[i, u],
            near_sem.at[0, i, u],
            near_sem.at[1, i, u],
            head=at_x(toward(u)),
        )

    def cross_copy(i):
        return remote(
            cross_out.at[i],
            cross_buf.at[i],
            cross_sem.at[0, i],
            cross_sem.at[1, i],
            head=other,
        )

    def spread_copy(i, step):
        place = lax.rem(c + step, N_CTX)
        return remote(
            slab.at[i, pl.ds(place * PIECE, PIECE)],
            out_ref.at[i, pl.ds(c * PIECE, PIECE)],
            spread_sem.at[0, i],
            spread_sem.at[1, i],
            ctx=place,
        )

    def own_copy(i):
        return pltpu.make_async_copy(
            slab.at[i, pl.ds(c * PIECE, PIECE)],
            out_ref.at[i, pl.ds(c * PIECE, PIECE)],
            spread_sem.at[1, i],
        )

    def far_stage(i):
        multiply(2, i)

        @pl.when(i == 0)
        def _():
            pl.semaphore_wait(barrier, 2 + 1 + N_CTX - 1)

        for u in range(2):
            far_copy(i, u).start()

    def side_stage(i):
        multiply(1, i)
        side_copy(i, 0).start()
        multiply(-1, i)
        side_copy(i, 1).start()

    def near_stage(i):
        for u in range(2):
            far_copy(i, u).wait_recv()
            near_out[i, u] = (
                partial[column(toward(u)), i, u].astype(jnp.float32)
                + far_buf[i, u].astype(jnp.float32)
            ).astype(jnp.bfloat16)
            near_copy(i, u).start()

    def own_stage(i):
        multiply(0, i)
        for u in range(2):
            side_copy(i, u).wait_recv()
            near_copy(i, u).wait_recv()

            def total(side):
                return (
                    partial[x, i, u, side].astype(jnp.float32)
                    + near_buf[i, u, side].astype(jnp.float32)
                    + side_buf[i, u, side].astype(jnp.float32)
                )

            cross_out[i, u] = total(1 - y).astype(jnp.bfloat16)
            keep[i, u] = total(y)
        cross_copy(i).start()

    def last_stage(i):
        cross_copy(i).wait_recv()
        for u in range(2):
            done = (keep[i, u] + cross_buf[i, u].astype(jnp.float32)).astype(
                jnp.bfloat16
            )
            slab[i, :, u * HALF : (u + 1) * HALF] = lax.dot_general(
                pick[...],
                done,
                (((1,), (1,)), ((), ())),
                preferred_element_type=jnp.float32,
            ).astype(jnp.bfloat16)
        own_copy(i).start()
        for step in range(1, N_CTX):
            spread_copy(i, step).start()

    stages = ((far_stage, 0), (side_stage, 1), (near_stage, 2), (own_stage, 4), (last_stage, 5))

    @pl.loop(0, CHUNKS + 5)
    def _(t):
        for stage, delay in stages:

            @pl.when((t >= delay) & (t < delay + CHUNKS))
            def _():
                stage(t - delay)

    @pl.loop(0, CHUNKS)
    def _(i):
        for u in range(2):
            far_copy(i, u).wait_send()
            side_copy(i, u).wait_send()
            near_copy(i, u).wait_send()
        cross_copy(i).wait_send()
        sent = slab.at[i, pl.ds(0, (N_CTX - 1) * PIECE)]
        pltpu.make_async_copy(sent, sent, spread_sem.at[0, i]).wait()
        pltpu.make_async_copy(out_ref.at[i], out_ref.at[i], spread_sem.at[1, i]).wait()


def project(owners, out_weight, context):
    vmem = pl.BlockSpec(memory_space=pltpu.VMEM)
    hbm = pl.BlockSpec(memory_space=pl.ANY)
    slots = N_CTX * PIECE
    unit = (CHUNKS, 2, 2, HALF, ROWS)
    half_unit = (CHUNKS, 2, HALF, ROWS)
    dma = pltpu.SemaphoreType.DMA
    return pl.pallas_call(
        project_kernel,
        out_shape=jax.ShapeDtypeStruct((CHUNKS, slots, CHUNK), jnp.bfloat16),
        in_specs=[pl.BlockSpec(memory_space=pltpu.SMEM), hbm, vmem],
        out_specs=hbm,
        scratch_shapes=[
            pltpu.VMEM((N_X, CHUNKS, 2, CHUNK, HEADS * HEAD_SIZE), jnp.bfloat16),
            pltpu.VMEM((N_X,) + unit, jnp.bfloat16),
            pltpu.VMEM(unit, jnp.bfloat16),
            pltpu.VMEM(unit, jnp.bfloat16),
            pltpu.VMEM(unit, jnp.bfloat16),
            pltpu.VMEM(unit, jnp.bfloat16),
            pltpu.VMEM(half_unit, jnp.bfloat16),
            pltpu.VMEM(half_unit, jnp.bfloat16),
            pltpu.VMEM(half_unit, jnp.float32),
            pltpu.VMEM((slots, ROWS), jnp.bfloat16),
            pltpu.VMEM((CHUNKS, slots, CHUNK), jnp.bfloat16),
            dma((N_X, CHUNKS)),
            dma((2, CHUNKS, 2)),
            dma((2, CHUNKS, 2)),
            dma((2, CHUNKS, 2)),
            dma((2, CHUNKS)),
            dma((2, CHUNKS)),
        ],
        compiler_params=pltpu.CompilerParams(
            collective_id=1, has_side_effects=True, vmem_limit_bytes=VMEM_LIMIT
        ),
        name="project",
    )(owners, out_weight, context)


def per_device(queries, keys, values, out_weight, doc_lengths, owners):
    context = attention(doc_lengths, queries, keys, values)
    blocks = out_weight.reshape(N_X, 2, CHUNKS, CHUNK, out_weight.shape[1])
    arrived = project(owners[:, 0], blocks, context)
    return jnp.swapaxes(arrived, 1, 2).reshape(CHUNKS * CHUNK, N_CTX * PIECE)


def solution(mesh):
    in_specs = (P("ctx", "head"), P("ctx", "head"), P("ctx", "head"), P(None, "head"), P(), P())
    out_specs = P("head", "ctx")
    return jax.shard_map(
        per_device, mesh=mesh, in_specs=in_specs, out_specs=out_specs, check_vma=False
    )
```

time: 448 us -> 83.2 us (0.19)
  waiting for transfers between devices: 252 us -> 0 us
  matrix products: 141 us -> 0 us
  Pallas kernels: 0 us -> 80.8 us
  other arithmetic: 24.2 us -> 0 us
  between operations: 13.2 us -> 0.02 us
  starting transfers between devices: 9.54 us -> 0 us
  local copies, waits for them, and re-layouts: 7.97 us -> 2.28 us
    reduce_scatter x1 -> x0, waiting for transfers between devices: 168 us -> none  [project(): lax.psum_scatter(lax.dot_general(out_weight, context, (((1,), (1,)), ((),...]
    dot_general x18 -> x0, matrix products: 141 us -> none  [the longest x8 65.4 us: one_tile(): jnp.einsum('rkgn,nkd->rkgd', weights.astype(jnp.bfloat16), value_block, p...]
    pallas_call x0 -> x2, Pallas kernels: none -> 80.8 us  [the longest x1 65.2 us: project(): pl.pallas_call(project_kernel, out_shape=jax.ShapeDtypeStruct((CHUNKS, sl...]
    all_gather x2 -> x0, waiting for transfers between devices: 67.4 us -> none  [the longest x1 47.4 us: attend(): key_piece = lax.all_gather(keys, 'ctx', axis=0, tiled=True)]
    reduce_sum x18 -> x0, other arithmetic: 17 us -> none  [the longest x8 16.1 us: one_tile(): new_sum = running_sum * factor + jnp.sum(weights, axis=-1)]
    all_to_all x1 -> x0, waiting for transfers between devices: 15.9 us -> none  [per_device(): lax.all_to_all(outgoing, 'ctx', split_axis=0, concat_axis=0, tiled=True)]
    all_to_all x1 -> x0, starting transfers between devices: 9.46 us -> none  [per_device(): lax.all_to_all(outgoing, 'ctx', split_axis=0, concat_axis=0, tiled=True)]
  transfers between devices with their start and end apart: 4 -> 0, of which waited for: 4 -> 0; matrix products, arithmetic and copies ran while one was open for 1% -> 0% of each run, Pallas kernels for 0% -> 0%
where the time goes in v1:
time: 83.2 us; the launch traced here: 83.1 us
  Pallas kernels  80.8 us (97%)
  local copies, waits for them, and re-layouts  2.28 us (3%)
    pallas_call x1, Pallas kernels, project(): pl.pallas_call(project_kernel, out_shape=jax.ShapeDtypeStruct((CHUNKS, sl...  65.2 us
    pallas_call x1, Pallas kernels, attention(): pl.pallas_call(attention_kernel, out_shape=jax.ShapeDtypeStruct((HEADS *...  15.6 us
    transpose x1, local copies, waits for them, and re-layouts, per_device(): return jnp.swapaxes(arrived, 1, 2).reshape(CHUNKS * CHUNK, N_CTX * PIECE)  2.28 us

profile of v1, /device:TPU:1, one launch (start us, length us, event | category | flops | bytes accessed | tf_op | source)
XLA Modules:
  0.0 83.1 jit_solution(16552572763124891922)
XLA Ops:
  0.0 15.6 %attention.1.ctx_ref = bf16[1024,256]{1,0:T(8,128)(2,1)} custom-call(s32[16]{0:T(128)} %lengths.1, bf16[256,1024]{1,0:T(8,128)(2,1)} %q_ref.1, bf16[256,128]{1,0:T(8,128)(2,1)} %k_ref.1, bf16[256,128]{1,0:T(8,128)(2,1)} %v_ref.1), custom_call_target="tpu_custom_call" | custom-call | tf_op jit(solution)/shard_map/attention/pallas_call | solution.py:227
  15.6 65.2 %project.1 = bf16[4,512,256]{2,1,0:T(8,128)(2,1)} custom-call(s32[128]{0:T(128)} %bitcast.6, bf16[4,2,4,256,1024]{4,3,2,1,0:T(8,128)(2,1)} %bitcast.4, bf16[1024,256]{1,0:T(8,128)(2,1)} %attention.1.ctx_ref), custom_call_target="tpu_custom_call" | custom-call | tf_op jit(solution)/shard_map/project/pallas_call | solution.py:468
  80.8 2.3 %copy.7 = bf16[4,256,512]{2,1,0:T(8,128)(2,1)} copy(bf16[4,256,512]{1,2,0:T(8,128)(2,1)} %bitcast.5) | data formatting | bytes 2097152 | tf_op jit(solution)/shard_map/transpose | solution.py:503

commit v2 on v1

--- a/solution.py
+++ b/solution.py
@@ -17,10 +17,11 @@
 ROWS = 256
 HEADS = 8
 BACK = 4
+EARLY = 5
 KEYS = (BACK + 1) * ROWS
-CHUNKS = 4
-CHUNK = 256
-HALF = 128
+CHUNKS = 8
+CHUNK = 128
+HALF = 64
 MASKED = -1e30
 VMEM_LIMIT = 60 * 1024 * 1024
 
@@ -43,7 +44,20 @@
 
 
 def attention_kernel(
-    lengths, q_ref, k_ref, v_ref, o_ref, kbuf, vbuf, vt, bias, send_sem, recv_sem
+    lengths,
+    q_ref,
+    k_ref,
+    v_ref,
+    o_ref,
+    kbuf,
+    vbuf,
+    vt,
+    bias,
+    tops,
+    totals,
+    mixes,
+    send_sem,
+    recv_sem,
 ):
     c = lax.axis_index("ctx")
     core = lax.rem(c, 2)
@@ -51,15 +65,14 @@
 
     barrier = pltpu.get_barrier_semaphore()
     signal(barrier, ctx=mate)
-    for far in (2, 4):
-
-        @pl.when(c + far < N_CTX)
-        def _():
-            signal(barrier, ctx=c + far)
-
-        @pl.when(c >= far)
-        def _():
-            signal(barrier, ctx=c - far)
+
+    @pl.when(c + 2 < N_CTX)
+    def _():
+        signal(barrier, ctx=c + 2)
+
+    @pl.when(c >= 2)
+    def _():
+        signal(barrier, ctx=c - 2)
 
     def slot(buf, back):
         return buf.at[pl.ds((BACK - back) * ROWS, ROWS)]
@@ -89,22 +102,21 @@
         allowed = (key_pos >= low) & (key_pos <= pos)
         bias[at : at + ROWS, :] = jnp.where(allowed, 0.0, MASKED)
 
-    count = 1
-    for far in (2, 4):
-        count = count + (c + far < N_CTX).astype(jnp.int32)
-        count = count + (c >= far).astype(jnp.int32)
+    forward = c + 2 < N_CTX
+    relayed = (c >= 2) & forward
+    count = 1 + forward.astype(jnp.int32) + (c >= 2).astype(jnp.int32)
     pl.semaphore_wait(barrier, count)
 
-    def far_copies(far):
+    def next_copies(source, back):
         return [
             remote(
-                own,
-                slot(buf, far),
-                send_sem.at[far // 2 - 1, i],
-                recv_sem.at[far - 1, i],
-                ctx=c + far,
+                source[i],
+                slot(buf, back),
+                send_sem.at[back // 2 - 1, i],
+                recv_sem.at[back - 1, i],
+                ctx=c + 2,
             )
-            for i, (own, buf) in enumerate(((k_ref, kbuf), (v_ref, vbuf)))
+            for i, buf in enumerate((kbuf, vbuf))
         ]
 
     def mate_copies(source, back):
@@ -119,85 +131,117 @@
             for i, buf in enumerate((kbuf, vbuf))
         ]
 
+    near_blocks = (slot(kbuf, 2), slot(vbuf, 2))
+    own_next = next_copies((k_ref, v_ref), 2)
+    relay_next = next_copies(near_blocks, 4)
     first_even = mate_copies((k_ref, v_ref), 1)
-    first_odd = mate_copies((slot(kbuf, 2), slot(vbuf, 2)), 1)
-    second_even = mate_copies((slot(kbuf, 2), slot(vbuf, 2)), 3)
+    first_odd = mate_copies(near_blocks, 1)
+    second_even = mate_copies(near_blocks, 3)
     second_odd = mate_copies((slot(kbuf, 4), slot(vbuf, 4)), 3)
+
+    @pl.when(forward)
+    def _():
+        for copy in own_next:
+            copy.start()
 
     @pl.when(core == 0)
     def _():
         for copy in first_even:
             copy.start()
 
-    for far in (2, 4):
-
-        @pl.when(c + far < N_CTX)
-        def _():
-            for copy in far_copies(far):
-                copy.start()
+    factor = math.log2(math.e) / math.sqrt(HEAD_SIZE)
+
+    def turn(low_key, high_key):
+        vt[:, low_key:high_key] = vbuf[low_key:high_key, :].T
+
+    def attend(low_key, high_key, heads, first=False, last=False):
+        @pl.loop(*heads)
+        def _(head):
+            at = pl.multiple_of(head * HEAD_SIZE, HEAD_SIZE)
+            scores = lax.dot_general(
+                kbuf[low_key:high_key, :],
+                q_ref[:, pl.ds(at, HEAD_SIZE)],
+                (((1,), (1,)), ((), ())),
+                preferred_element_type=jnp.float32,
+            )
+            scores = scores + bias[low_key:high_key, :]
+            top = jnp.max(scores, axis=0, keepdims=True)
+            if not first:
+                top = jnp.maximum(top, tops[head])
+            weights = jnp.exp2((scores - top) * factor)
+            total = jnp.sum(weights, axis=0, keepdims=True)
+            mixed = jnp.dot(
+                vt[:, low_key:high_key],
+                weights.astype(jnp.bfloat16),
+                preferred_element_type=jnp.float32,
+            )
+            if not first:
+                shrink = jnp.exp2((tops[head] - top) * factor)
+                total = total + totals[head] * shrink
+                mixed = mixed + mixes[head] * shrink
+            if last:
+                o_ref[pl.ds(at, HEAD_SIZE), :] = (mixed / total).astype(jnp.bfloat16)
+            else:
+                tops[head] = top
+                totals[head] = total
+                mixes[head] = mixed
+
+    turn(BACK * ROWS, KEYS)
+    attend(BACK * ROWS, KEYS, (0, HEADS), first=True)
 
     @pl.when(c >= 2)
     def _():
-        for copy in far_copies(2):
-            copy.wait_recv()
-
-        @pl.when(core == 1)
-        def _():
-            for copy in first_odd:
-                copy.start()
-
-        @pl.when(core == 0)
-        def _():
-            for copy in second_even:
-                copy.start()
-
-    @pl.when(c >= 4)
-    def _():
-        for copy in far_copies(4):
-            copy.wait_recv()
-
-        @pl.when(core == 1)
-        def _():
-            for copy in second_odd:
-                copy.start()
+        for i in range(2):
+            own_next[i].wait_recv()
+
+            @pl.when(forward)
+            def _():
+                relay_next[i].start()
+
+            @pl.when(core == 1)
+            def _():
+                first_odd[i].start()
+
+            @pl.when(core == 0)
+            def _():
+                second_even[i].start()
 
     @pl.when(c >= 1)
     def _():
         for copy in first_odd:
             copy.wait_recv()
 
+    turn(2 * ROWS, BACK * ROWS)
+    attend(2 * ROWS, BACK * ROWS, (0, EARLY))
+
+    @pl.when(c >= 4)
+    def _():
+        for i in range(2):
+            relay_next[i].wait_recv()
+
+            @pl.when(core == 1)
+            def _():
+                second_odd[i].start()
+
+    attend(2 * ROWS, BACK * ROWS, (EARLY, HEADS))
+
     @pl.when(c >= 3)
     def _():
         for copy in second_odd:
             copy.wait_recv()
 
-    vt[...] = vbuf[...].T
-    factor = math.log2(math.e) / math.sqrt(HEAD_SIZE)
-
-    @pl.loop(0, HEADS)
-    def _(head):
-        at = pl.multiple_of(head * HEAD_SIZE, HEAD_SIZE)
-        scores = lax.dot_general(
-            kbuf[...],
-            q_ref[:, pl.ds(at, HEAD_SIZE)],
-            (((1,), (1,)), ((), ())),
-            preferred_element_type=jnp.float32,
-        )
-        scores = scores + bias[...]
-        top = jnp.max(scores, axis=0, keepdims=True)
-        weights = jnp.exp2((scores - top) * factor)
-        total = jnp.sum(weights, axis=0, keepdims=True)
-        mixed = jnp.dot(
-            vt[...], weights.astype(jnp.bfloat16), preferred_element_type=jnp.float32
-        )
-        o_ref[pl.ds(at, HEAD_SIZE), :] = (mixed / total).astype(jnp.bfloat16)
-
-    for far in (2, 4):
-
-        @pl.when(c + far < N_CTX)
-        def _():
-            for copy in far_copies(far):
-                copy.wait_send()
+    turn(0, 2 * ROWS)
+    attend(0, 2 * ROWS, (0, HEADS), last=True)
+
+    @pl.when(forward)
+    def _():
+        for copy in own_next:
+            copy.wait_send()
+
+    @pl.when(relayed)
+    def _():
+        for copy in relay_next:
+            copy.wait_send()
 
     @pl.when(core == 0)
     def _():
@@ -234,6 +278,9 @@
             pltpu.VMEM((KEYS, HEAD_SIZE), jnp.bfloat16),
             pltpu.VMEM((HEAD_SIZE, KEYS), jnp.bfloat16),
             pltpu.VMEM((KEYS, ROWS), jnp.float32),
+            pltpu.VMEM((HEADS, 1, ROWS), jnp.float32),
+            pltpu.VMEM((HEADS, 1, ROWS), jnp.float32),
+            pltpu.VMEM((HEADS, HEAD_SIZE, ROWS), jnp.float32),
             pltpu.SemaphoreType.DMA((4, 2)),
             pltpu.SemaphoreType.DMA((4, 2)),
         ],
@@ -312,15 +359,15 @@
         place = column(step)
         load(place, i).wait()
 
-        @pl.loop(0, 2)
-        def _(side):
-            block = jnp.dot(
-                weights[place, i, side],
-                ctx_ref[...],
-                preferred_element_type=jnp.float32,
-            ).astype(jnp.bfloat16)
-            partial[place, i, 0, side] = block[:HALF]
-            partial[place, i, 1, side] = block[HALF:]
+        block = jnp.dot(
+            weights[place, i].reshape(2 * CHUNK, HEADS * HEAD_SIZE),
+            ctx_ref[...],
+            preferred_element_type=jnp.float32,
+        ).astype(jnp.bfloat16)
+        for side in range(2):
+            for u in range(2):
+                at = side * CHUNK + u * HALF
+                partial[place, i, u, side] = block[at : at + HALF]
 
     def toward(u):
         return 2 * u - 1
@@ -422,16 +469,13 @@
 
     def last_stage(i):
         cross_copy(i).wait_recv()
-        for u in range(2):
-            done = (keep[i, u] + cross_buf[i, u].astype(jnp.float32)).astype(
-                jnp.bfloat16
-            )
-            slab[i, :, u * HALF : (u + 1) * HALF] = lax.dot_general(
-                pick[...],
-                done,
-                (((1,), (1,)), ((), ())),
-                preferred_element_type=jnp.float32,
-            ).astype(jnp.bfloat16)
+        done = (keep[i] + cross_buf[i].astype(jnp.float32)).astype(jnp.bfloat16)
+        slab[i] = lax.dot_general(
+            pick[...],
+            done.reshape(CHUNK, ROWS),
+            (((1,), (1,)), ((), ())),
+            preferred_element_type=jnp.float32,
+        ).astype(jnp.bfloat16)
         own_copy(i).start()
         for step in range(1, N_CTX):
             spread_copy(i, step).start()

time: 83.2 us -> 78.1 us (0.939)
  Pallas kernels: 80.8 us -> 75.6 us
    pallas_call x1, Pallas kernels: 65.2 us -> 58.7 us  [project(): pl.pallas_call(project_kernel, out_shape=jax.ShapeDtypeStruct((CHUNKS, sl...]
    pallas_call x1, Pallas kernels: 15.6 us -> 17 us  [attention(): pl.pallas_call(attention_kernel, out_shape=jax.ShapeDtypeStruct((HEADS *...]
where the time goes in v2:
time: 78.1 us; the launch traced here: 77.9 us
  Pallas kernels  75.6 us (97%)
  local copies, waits for them, and re-layouts  2.27 us (3%)
    pallas_call x1, Pallas kernels, project(): pl.pallas_call(project_kernel, out_shape=jax.ShapeDtypeStruct((CHUNKS, sl...  58.7 us
    pallas_call x1, Pallas kernels, attention(): pl.pallas_call(attention_kernel, out_shape=jax.ShapeDtypeStruct((HEADS *...  17 us
    transpose x1, local copies, waits for them, and re-layouts, per_device(): return jnp.swapaxes(arrived, 1, 2).reshape(CHUNKS * CHUNK, N_CTX * PIECE)  2.27 us

profile of v2, /device:TPU:1, one launch (start us, length us, event | category | flops | bytes accessed | tf_op | source)
XLA Modules:
  0.0 77.9 jit_solution(2727286178940404789)
XLA Ops:
  0.0 17.0 %attention.1.ctx_ref = bf16[1024,256]{1,0:T(8,128)(2,1)} custom-call(s32[16]{0:T(128)} %lengths.1, bf16[256,1024]{1,0:T(8,128)(2,1)} %q_ref.1, bf16[256,128]{1,0:T(8,128)(2,1)} %k_ref.1, bf16[256,128]{1,0:T(8,128)(2,1)} %v_ref.1), custom_call_target="tpu_custom_call" | custom-call | tf_op jit(solution)/shard_map/attention/pallas_call | solution.py:271
  17.0 58.7 %project.1 = bf16[8,512,128]{2,1,0:T(8,128)(2,1)} custom-call(s32[128]{0:T(128)} %bitcast.6, bf16[4,2,8,128,1024]{4,3,2,1,0:T(8,128)(2,1)} %bitcast.4, bf16[1024,256]{1,0:T(8,128)(2,1)} %attention.1.ctx_ref), custom_call_target="tpu_custom_call" | custom-call | tf_op jit(solution)/shard_map/project/pallas_call | solution.py:512
  75.6 2.3 %copy.7 = bf16[8,128,512]{2,1,0:T(8,128)(2,1)} copy(bf16[8,128,512]{1,2,0:T(8,128)(2,1)} %bitcast.5) | data formatting | bytes 2097152 | tf_op jit(solution)/shard_map/transpose | solution.py:547

commit v3 on v2

--- a/solution.py
+++ b/solution.py
@@ -43,8 +43,9 @@
     )
 
 
-def attention_kernel(
+def attend_rows(
     lengths,
+    prepare,
     q_ref,
     k_ref,
     v_ref,
@@ -63,17 +64,6 @@
     core = lax.rem(c, 2)
     mate = c + 1 - 2 * core
 
-    barrier = pltpu.get_barrier_semaphore()
-    signal(barrier, ctx=mate)
-
-    @pl.when(c + 2 < N_CTX)
-    def _():
-        signal(barrier, ctx=c + 2)
-
-    @pl.when(c >= 2)
-    def _():
-        signal(barrier, ctx=c - 2)
-
     def slot(buf, back):
         return buf.at[pl.ds((BACK - back) * ROWS, ROWS)]
 
@@ -104,8 +94,7 @@
 
     forward = c + 2 < N_CTX
     relayed = (c >= 2) & forward
-    count = 1 + forward.astype(jnp.int32) + (c >= 2).astype(jnp.int32)
-    pl.semaphore_wait(barrier, count)
+    prepare()
 
     def next_copies(source, back):
         return [
@@ -266,36 +255,24 @@
                 copy.wait_send()
 
 
-def attention(lengths, queries, keys, values):
-    vmem = pl.BlockSpec(memory_space=pltpu.VMEM)
-    return pl.pallas_call(
-        attention_kernel,
-        out_shape=jax.ShapeDtypeStruct((HEADS * HEAD_SIZE, ROWS), jnp.bfloat16),
-        in_specs=[pl.BlockSpec(memory_space=pltpu.SMEM), vmem, vmem, vmem],
-        out_specs=vmem,
-        scratch_shapes=[
-            pltpu.VMEM((KEYS, HEAD_SIZE), jnp.bfloat16),
-            pltpu.VMEM((KEYS, HEAD_SIZE), jnp.bfloat16),
-            pltpu.VMEM((HEAD_SIZE, KEYS), jnp.bfloat16),
-            pltpu.VMEM((KEYS, ROWS), jnp.float32),
-            pltpu.VMEM((HEADS, 1, ROWS), jnp.float32),
-            pltpu.VMEM((HEADS, 1, ROWS), jnp.float32),
-            pltpu.VMEM((HEADS, HEAD_SIZE, ROWS), jnp.float32),
-            pltpu.SemaphoreType.DMA((4, 2)),
-            pltpu.SemaphoreType.DMA((4, 2)),
-        ],
-        compiler_params=pltpu.CompilerParams(
-            collective_id=0, has_side_effects=True, vmem_limit_bytes=VMEM_LIMIT
-        ),
-        name="attention",
-    )(lengths, queries, keys, values)
-
-
-def project_kernel(
+def layer_kernel(
+    lengths,
     owners,
+    q_ref,
+    k_ref,
+    v_ref,
     w_ref,
+    out_ref,
     ctx_ref,
-    out_ref,
+    kbuf,
+    vbuf,
+    vt,
+    bias,
+    tops,
+    totals,
+    mixes,
+    send_sem,
+    recv_sem,
     weights,
     partial,
     far_buf,
@@ -343,17 +320,37 @@
         for i in range(CHUNKS):
             load(column(step), i).start()
 
-    row = lax.broadcasted_iota(jnp.int32, (N_CTX * PIECE, ROWS), 0)
-    col = lax.broadcasted_iota(jnp.int32, (N_CTX * PIECE, ROWS), 1)
-    lane = lax.broadcasted_iota(jnp.int32, (1, ROWS), 1)
-    wanted = jnp.zeros((1, ROWS), jnp.int32)
-    for piece in range(PIECES):
-        wanted = jnp.where(
-            (lane >= piece * PIECE) & (lane < (piece + 1) * PIECE),
-            owners[c * PIECES + piece] * PIECE + lane - piece * PIECE,
-            wanted,
-        )
-    pick[...] = (row == wanted).astype(jnp.float32).astype(jnp.bfloat16)
+    def prepare():
+        row = lax.broadcasted_iota(jnp.int32, (N_CTX * PIECE, ROWS), 0)
+        col = lax.broadcasted_iota(jnp.int32, (N_CTX * PIECE, ROWS), 1)
+        lane = lax.broadcasted_iota(jnp.int32, (1, ROWS), 1)
+        wanted = jnp.zeros((1, ROWS), jnp.int32)
+        for piece in range(PIECES):
+            wanted = jnp.where(
+                (lane >= piece * PIECE) & (lane < (piece + 1) * PIECE),
+                owners[c * PIECES + piece] * PIECE + lane - piece * PIECE,
+                wanted,
+            )
+        pick[...] = (row == wanted).astype(jnp.float32).astype(jnp.bfloat16)
+        pl.semaphore_wait(barrier, 2 + 1 + N_CTX - 1)
+
+    attend_rows(
+        lengths,
+        prepare,
+        q_ref,
+        k_ref,
+        v_ref,
+        ctx_ref,
+        kbuf,
+        vbuf,
+        vt,
+        bias,
+        tops,
+        totals,
+        mixes,
+        send_sem,
+        recv_sem,
+    )
 
     def multiply(step, i):
         place = column(step)
@@ -427,11 +424,6 @@
 
     def far_stage(i):
         multiply(2, i)
-
-        @pl.when(i == 0)
-        def _():
-            pl.semaphore_wait(barrier, 2 + 1 + N_CTX - 1)
-
         for u in range(2):
             far_copy(i, u).start()
 
@@ -502,19 +494,30 @@
         pltpu.make_async_copy(out_ref.at[i], out_ref.at[i], spread_sem.at[1, i]).wait()
 
 
-def project(owners, out_weight, context):
+def layer(lengths, owners, queries, keys, values, out_weight):
     vmem = pl.BlockSpec(memory_space=pltpu.VMEM)
     hbm = pl.BlockSpec(memory_space=pl.ANY)
+    smem = pl.BlockSpec(memory_space=pltpu.SMEM)
     slots = N_CTX * PIECE
     unit = (CHUNKS, 2, 2, HALF, ROWS)
     half_unit = (CHUNKS, 2, HALF, ROWS)
     dma = pltpu.SemaphoreType.DMA
     return pl.pallas_call(
-        project_kernel,
+        layer_kernel,
         out_shape=jax.ShapeDtypeStruct((CHUNKS, slots, CHUNK), jnp.bfloat16),
-        in_specs=[pl.BlockSpec(memory_space=pltpu.SMEM), hbm, vmem],
+        in_specs=[smem, smem, vmem, vmem, vmem, hbm],
         out_specs=hbm,
         scratch_shapes=[
+            pltpu.VMEM((HEADS * HEAD_SIZE, ROWS), jnp.bfloat16),
+            pltpu.VMEM((KEYS, HEAD_SIZE), jnp.bfloat16),
+            pltpu.VMEM((KEYS, HEAD_SIZE), jnp.bfloat16),
+            pltpu.VMEM((HEAD_SIZE, KEYS), jnp.bfloat16),
+            pltpu.VMEM((KEYS, ROWS), jnp.float32),
+            pltpu.VMEM((HEADS, 1, ROWS), jnp.float32),
+            pltpu.VMEM((HEADS, 1, ROWS), jnp.float32),
+            pltpu.VMEM((HEADS, HEAD_SIZE, ROWS), jnp.float32),
+            dma((4, 2)),
+            dma((4, 2)),
             pltpu.VMEM((N_X, CHUNKS, 2, CHUNK, HEADS * HEAD_SIZE), jnp.bfloat16),
             pltpu.VMEM((N_X,) + unit, jnp.bfloat16),
             pltpu.VMEM(unit, jnp.bfloat16),
@@ -534,16 +537,15 @@
             dma((2, CHUNKS)),
         ],
         compiler_params=pltpu.CompilerParams(
-            collective_id=1, has_side_effects=True, vmem_limit_bytes=VMEM_LIMIT
+            collective_id=0, has_side_effects=True, vmem_limit_bytes=VMEM_LIMIT
         ),
-        name="project",
-    )(owners, out_weight, context)
+        name="layer",
+    )(lengths, owners, queries, keys, values, out_weight)
 
 
 def per_device(queries, keys, values, out_weight, doc_lengths, owners):
-    context = attention(doc_lengths, queries, keys, values)
     blocks = out_weight.reshape(N_X, 2, CHUNKS, CHUNK, out_weight.shape[1])
-    arrived = project(owners[:, 0], blocks, context)
+    arrived = layer(doc_lengths, owners[:, 0], queries, keys, values, blocks)
     return jnp.swapaxes(arrived, 1, 2).reshape(CHUNKS * CHUNK, N_CTX * PIECE)
 
 

time: 78.1 us -> 75.5 us (0.967)
  Pallas kernels: 75.6 us -> 73.1 us
    pallas_call x2 -> x1, Pallas kernels: 75.6 us -> 73.1 us  [layer(): pl.pallas_call(layer_kernel, out_shape=jax.ShapeDtypeStruct((CHUNKS, slot...]
where the time goes in v3:
time: 75.5 us; the launch traced here: 75.4 us
  Pallas kernels  73.1 us (97%)
  local copies, waits for them, and re-layouts  2.27 us (3%)
    pallas_call x1, Pallas kernels, layer(): pl.pallas_call(layer_kernel, out_shape=jax.ShapeDtypeStruct((CHUNKS, slot...  73.1 us
    transpose x1, local copies, waits for them, and re-layouts, per_device(): return jnp.swapaxes(arrived, 1, 2).reshape(CHUNKS * CHUNK, N_CTX * PIECE)  2.27 us

profile of v3, /device:TPU:1, one launch (start us, length us, event | category | flops | bytes accessed | tf_op | source)
XLA Modules:
  0.0 75.4 jit_solution(5577722295149241949)
XLA Ops:
  0.0 73.1 %layer.1 = bf16[8,512,128]{2,1,0:T(8,128)(2,1)} custom-call(s32[16]{0:T(128)} %lengths.1, s32[128]{0:T(128)} %bitcast.6, bf16[256,1024]{1,0:T(8,128)(2,1)} %q_ref.1, bf16[256,128]{1,0:T(8,128)(2,1)} %k_ref.1, bf16[256,128]{1,0:T(8,128)(2,1)} %v_ref.1, bf16[4,2,8,128,1024]{4,3,2,1,0:T(8,128)(2,1)} %bitcast.4), custom_call_target="tpu_custom_call" | custom-call | tf_op jit(solution)/shard_map/layer/pallas_call | solution.py:505
  73.1 2.3 %copy.7 = bf16[8,128,512]{2,1,0:T(8,128)(2,1)} copy(bf16[8,128,512]{1,2,0:T(8,128)(2,1)} %bitcast.5) | data formatting | bytes 2097152 | tf_op jit(solution)/shard_map/transpose | solution.py:549
